TPU v7x, 256 devices: a whole 4x4x8 slice. The times are simulated.
256 devices in a mesh: row: 32 (over y, z), col: 8 (over x, core).
Axes of the slice: x: 4, y: 4, z: 8, core: 2. Of those that a mesh axis runs over, the one named last changes fastest.
Arguments:
- tail_factor: bfloat16 [131072, 1024], P('row'), may hold values from -0.015625 to 0.015625
- tail_solution: bfloat16 [131072, 2048], P('row', 'col'), may hold values from -6 to 6
- panel_rhs: float32 [1024, 2048], P('row', 'col'), may hold values from -6 to 6
- panel_factor: bfloat16 [3, 512, 512], P(None, 'col'), as said below
Outputs:
- panel_solution: float32 [1024, 2048], P(None, 'col')
Inputs may be any that keep to these rules, and one draw needn't show every extreme that they name: panel_factor[0] and panel_factor[1] are unit lower triangular: ones on the diagonal and zeros above it.
All inputs are finite; a program needn't handle non-finite values.
Results may differ from a plain program's by a relative error of at most 0.0003.
Values may be sent and summed in bfloat16 or wider, within the bound.
A program may use at most 64 MiB of HBM per device.

v0:
```python
import jax
import jax.numpy as jnp
from jax import lax
from jax.sharding import PartitionSpec as P


def solve_block(lower, rhs):
    return jax.scipy.linalg.solve_triangular(lower, rhs, trans=1, lower=True, unit_diagonal=True)


def local_update(tail_factor, tail_solution):
    return lax.dot_general(
        tail_factor, tail_solution, (((0,), (0,)), ((), ())), preferred_element_type=jnp.float32
    )


def shards(tail_factor, tail_solution, panel_rhs, panel_factor):
    blocks = lax.all_gather(panel_factor, "col", axis=1, tiled=True).astype(jnp.float32)
    panel_width = tail_factor.shape[1]
    half_width = panel_width // 2
    whole_rhs = lax.all_gather(panel_rhs, "row", axis=0, tiled=True)
    term = local_update(tail_factor, tail_solution)
    summed = lax.psum(term, "row")
    reduced = whole_rhs - summed
    later = solve_block(blocks[1], reduced[half_width:])
    earlier_rhs = reduced[:half_width]
    adjusted = earlier_rhs - jnp.dot(
        blocks[2].T, later, precision=lax.Precision.HIGHEST, preferred_element_type=jnp.float32
    )
    earlier = solve_block(blocks[0], adjusted)
    return jnp.concatenate([earlier, later], axis=0)


def solution(mesh):
    return jax.shard_map(
        shards,
        mesh=mesh,
        in_specs=(P("row", None), P("row", "col"), P("row", "col"), P(None, "col", None)),
        out_specs=P(None, "col"),
        check_vma=False,
    )
```

profile of v0, /device:TPU:8, one launch (start us, length us, event | category | flops | bytes accessed | tf_op | source)
XLA Modules:
  0.0 404.7 jit_solution(5566970083653288185)
XLA Ops:
  6.5 1.6 copy-done
  8.1 6.7 %fusion.49 = f32[1024,256]{1,0:T(8,128)} fusion(bf16[4096,1024]{1,0:T(8,128)(2,1)} %param.6, bf16[4096,256]{1,0:T(8,128)(2,1)S(1)} %copy-done), kind=kOutput, calls=%fused_computation.78 | convolution fusion | flops 2147483648 | bytes 11534336 | tf_op jit(solution)/shard_map/dot_general | solution.py:12
  16.4 150.7 %all-reduce.2.cloned.1.call-done = f32[1024,256]{1,0:T(8,128)} async-done(((f32[1024,256]{1,0:T(8,128)}), f32[1024,256]{1,0:T(8,128)}) %all-reduce.2.cloned.1.call-update) | async-done | bytes 1048592 | tf_op jit(solution)/shard_map/psum | solution.py:23
  167.1 76.4 %all-gather.5.cloned.1.call-done = f32[1024,256]{1,0:T(8,128)} async-done(((f32[32,256]{1,0:T(8,128)}), f32[1024,256]{1,0:T(8,128)}) %all-gather.5.cloned.1.call-update) | async-done | bytes 1048592 | tf_op jit(solution)/shard_map/all_gather | solution.py:21
  243.5 1.7 sub.6
  245.2 25.6 %all-gather.3.cloned.1.call-done = bf16[3,512,512]{2,1,0:T(8,128)(2,1)} async-done(((bf16[3,64,512]{2,1,0:T(8,128)(2,1)}), bf16[3,512,512]{2,1,0:T(8,128)(2,1)}) %all-gather.3.cloned.1.call-update) | async-done | bytes 1572880 | tf_op jit(solution)/shard_map/all_gather | solution.py:18
  270.8 1.8 convert_element_type.3
  272.6 1.6 convert_add_fusion.1
  274.2 11.3 %while.4 = (s32[]{:T(128)}, f32[512,512]{1,0:T(8,128)}, s32[4,2]{0,1:T(2,128)S(1)}, f32[4,128,128]{2,1,0:T(8,128)S(1)}, s32[]{:T(128)}) while((s32[]{:T(128)}, f32[512,512]{1,0:T(8,128)}, s32[4,2]{0,1:T(2,128)S(1)}, f32[4,128,128]{2,1,0:T(8,128)S(1)}, s32[]{:T(128)}) %tuple.36), condition=%wide.while_cond, body=%wide.while_body.sunk | while | flops 2 | bytes 131181 | solution.py:8
  274.9 2.2 bitcast_dynamic-update-slice_fusion.4
  277.7 2.2 bitcast_dynamic-update-slice_fusion.4
  280.6 2.2 bitcast_dynamic-update-slice_fusion.4
  283.4 2.1 bitcast_dynamic-update-slice_fusion.4
  286.3 40.1 %custom-call.4 = f32[4,128,128]{1,2,0:T(8,128)S(1)} custom-call(f32[4,128,128]{2,1,0:T(8,128)} %copy-done.4), custom_call_target="InvertDiagBlocksLowerTriangular" | custom-call | tf_op jit(solution)/shard_map/jit(_solve_triangular)/triangular_solve | solution.py:8
  331.8 1.4 convolution_subtract_fusion.2
  333.2 1.8 fusion.40
  335.7 13.8 %while.5 = (s32[]{:T(128)}, f32[512,512]{1,0:T(8,128)}, s32[4,2]{0,1:T(2,128)S(1)}, f32[4,128,128]{2,1,0:T(8,128)}, s32[]{:T(128)}) while((s32[]{:T(128)}, f32[512,512]{1,0:T(8,128)}, s32[4,2]{0,1:T(2,128)S(1)}, f32[4,128,128]{2,1,0:T(8,128)}, s32[]{:T(128)}) %tuple.48), condition=%wide.while_cond.clone, body=%wide.while_body.clone.sunk | while | flops 2 | bytes 132705 | solution.py:8
  336.3 2.8 bitcast_dynamic-update-slice_fusion.5
  339.8 2.9 bitcast_dynamic-update-slice_fusion.5
  343.3 2.9 bitcast_dynamic-update-slice_fusion.5
  346.8 2.8 bitcast_dynamic-update-slice_fusion.5
  349.5 40.7 %custom-call.5 = f32[4,128,128]{1,2,0:T(8,128)} custom-call(f32[4,128,128]{2,1,0:T(8,128)} %get-tuple-element.21), custom_call_target="InvertDiagBlocksLowerTriangular" | custom-call | tf_op jit(solution)/shard_map/jit(_solve_triangular)/triangular_solve | solution.py:8
  390.3 1.9 fusion
  395.5 1.4 convolution_subtract_fusion
  (48 shorter events, 17.9 us)
Async XLA Ops:
  6.5 1.6 copy-start
  6.5 160.5 %all-reduce.2.cloned.1.call-start = ((), (), s32[]{:S(2)}) async-start(), calls=%async_computation.2 | async-start | bytes 2097152 | tf_op jit(solution)/shard_map/psum | solution.py:23
  14.9 228.6 %all-gather.5.cloned.1.call-start = ((), (), s32[]{:S(2)}) async-start(), calls=%async_computation.1 | async-start | bytes 1081344 | tf_op jit(solution)/shard_map/all_gather | solution.py:21
  15.6 255.2 %all-gather.3.cloned.1.call-start = ((), (), s32[]{:S(2)}) async-start(), calls=%async_computation | async-start | bytes 1769472 | tf_op jit(solution)/shard_map/all_gather | solution.py:18
  285.5 0.7 copy-start.4
  326.4 0.7 copy-start.3
  390.3 1.9 copy-start.2
  392.2 5.0 %copy-start.1 = (f32[128,256]{1,0:T(8,128)S(1)}, f32[128,256]{1,0:T(8,128)}, u32[]{:S(2)}) copy-start(f32[128,256]{1,0:T(8,128)} %fusion.40) | copy-start | bytes 393220
Sparse Core Ops, SparseCore 0:
  15.0 152.0 all-reduce.1
  169.7 73.7 all-gather.4
  245.3 25.4 all-gather.2
where the time goes:
time: 407 us; the launch traced here: 405 us
  waiting for transfers between devices  254 us (62%)
  other arithmetic  87 us (21%)
  local copies, waits for them, and re-layouts  28.6 us (7%)
  matrix products  21.6 us (5%)
  between operations  13.3 us (3%)
    psum x1, waiting for transfers between devices, shards(): summed = lax.psum(term, 'row')  151 us
    another operation x5, other arithmetic, solve_block(): jax.scipy.linalg.solve_triangular(lower, rhs, trans=1, lower=True, unit_d...  82.4 us
    all_gather x1, waiting for transfers between devices, shards(): whole_rhs = lax.all_gather(panel_rhs, 'row', axis=0, tiled=True)  76.4 us
    another operation x27, local copies, waits for them, and re-layouts, solve_block(): jax.scipy.linalg.solve_triangular(lower, rhs, trans=1, lower=True, unit_d...  25.8 us
    all_gather x1, waiting for transfers between devices, shards(): lax.all_gather(panel_factor, 'col', axis=1, tiled=True).astype(jnp.float32)  25.6 us
    another operation x14, matrix products, solve_block(): jax.scipy.linalg.solve_triangular(lower, rhs, trans=1, lower=True, unit_d...  13 us
  transfers between devices with their start and end apart: 3, of which 3 were waited for; matrix products, arithmetic and copies ran while one was open for 0% of the time, Pallas kernels for 0%

commit v1 on v0

v1 whole, which is shorter than its diff:
```python
import jax
import jax.numpy as jnp
from jax import lax
from jax.experimental import pallas as pl
from jax.experimental.pallas import tpu as pltpu
from jax.sharding import PartitionSpec as P

MESH = pl.DeviceIdType.MESH
F32 = jnp.float32
BF16 = jnp.bfloat16

NY, NZ, NX = 4, 8, 4
BLOCK = 512
WINDOW = 2 * BLOCK
PIECE = 256
PIECES = WINDOW // PIECE
SUB = 128
SUBS = BLOCK // SUB


def split(x):
    high = x.astype(BF16)
    return high, (x - high.astype(F32)).astype(BF16)


def mm(a, b):
    return jnp.dot(a, b, preferred_element_type=F32)


def mm_exact(a, b):
    high, low = split(a)
    return mm(high, b) + mm(low, b)


def mm_split(a, b):
    a_high, a_low = split(a)
    b_high, b_low = split(b)
    return mm(a_high, b_high) + (mm(a_low, b_high) + mm(a_high, b_low))


def unit_inverse(lower):
    row = lax.broadcasted_iota(jnp.int32, (SUB, SUB), 0)
    col = lax.broadcasted_iota(jnp.int32, (SUB, SUB), 1)
    block = lower.astype(F32)

    def below(size):
        inside = (row // (2 * size) == col // (2 * size)) & (row // size == col // size + 1)
        return jnp.where(inside, block, 0.0)

    inverse = jnp.where(row == col, 1.0, 0.0) - below(1)
    size = 2
    while size < SUB:
        inverse = inverse - mm_split(mm_exact(inverse, below(size).astype(BF16)), inverse)
        size *= 2
    return inverse


def kernel(
    a_hbm, b_hbm, rhs_hbm, panel_hbm, out_ref,
    a_v, b_v, bt, rhs_v, place, ut, yrecv, w, zrecv, g, lf, blk, dinv, mh, ml,
    load_sem, y_s, y_r, z_s, z_r, gz_s, gz_r, gy_s, gy_r,
    px_s, px_r, pc_s, pc_r, dx_s, dx_r, dc_s, dc_r,
):
    row, col = lax.axis_index("row"), lax.axis_index("col")
    y, z = row // NZ, row % NZ
    x, core = col // 2, col % 2
    other = x * 2 + (1 - core)
    right = lax.rem(y + 1, NY) * NZ + z
    left = lax.rem(y + NY - 1, NY) * NZ + z
    depth = a_hbm.shape[0]
    width = b_hbm.shape[1]
    group = width // NY
    half = group // 2
    own = width // (NY * NZ)

    def remote(src, dst, send, recv, r, c):
        return pltpu.make_async_remote_copy(
            src_ref=src, dst_ref=dst, send_sem=send, recv_sem=recv,
            device_id=(r, c), device_id_type=MESH,
        )

    def z_peer(d):
        return y * NZ + lax.rem(z + d, NZ)

    def x_peer(d):
        return lax.rem(x + d, NX) * 2 + core

    loads = [pltpu.make_async_copy(b_hbm, b_v, load_sem.at[0])]
    for n in range(PIECES - 1, -1, -1):
        loads.append(
            pltpu.make_async_copy(a_hbm.at[:, PIECE * n : PIECE * (n + 1)], a_v.at[n], load_sem.at[1 + n])
        )
    loads.append(pltpu.make_async_copy(rhs_hbm, rhs_v, load_sem.at[5]))
    loads.append(pltpu.make_async_copy(panel_hbm, lf.at[:, col], load_sem.at[6]))
    for load in loads:
        load.start()

    barrier = pltpu.get_barrier_semaphore()

    def greet(r, c):
        pl.semaphore_signal(barrier, inc=1, device_id=(r, c), device_id_type=MESH)

    greet(left, col)
    greet(right, col)
    for d in range(1, NZ):
        greet(z_peer(d), col)
    for d in range(1, NX):
        greet(row, x_peer(d))
    greet(row, other)

    place[...] = jnp.zeros_like(place)
    loads[5].wait()
    place[pl.ds(pl.multiple_of(z * 32, 8), 32), :] = rhs_v[...]
    loads[0].wait()
    for k in range(0, depth, 512):
        bt[:, k : k + 512] = b_v[k : k + 512, :].T

    pl.semaphore_wait(barrier, 2 + (NZ - 1) + (NX - 1) + 1)

    for d in range(1, NX):
        remote(panel_hbm, lf.at[:, col], px_s.at[d - 1], px_r.at[d - 1], row, x_peer(d)).start()
    remote(panel_hbm, lf.at[:, col], pc_s.at[0], pc_r.at[0], row, other).start()

    def y_group(target):
        return pl.multiple_of(target // NZ * group, group)

    right_rows, left_rows = y_group(right), y_group(left)
    far_rows = pl.multiple_of(lax.rem(y + 2, NY) * group, group)
    own_rows = pl.multiple_of(y * group, group)

    def y_copy(n, slot):
        start = ((right_rows, 1), (far_rows, 0), (right_rows, 0), (left_rows, 0), (far_rows, 1), (left_rows, 1))[slot]
        src = ut.at[n, pl.ds(start[0] + start[1] * half, half), :]
        target = right if slot < 3 else left
        return remote(src, yrecv.at[n, slot], y_s.at[n, slot], y_r.at[n, slot], target, col)

    def update(step, carry):
        n = PIECES - 1 - step
        pltpu.make_async_copy(a_hbm.at[:, 0:PIECE], a_v.at[n], load_sem.at[1 + n]).wait()
        ut[n] = mm(bt[...], a_v[n])

        @pl.when(n == y)
        def _():
            ut[n] = ut[n] - place[...].T

        for slot in (1, 4, 0, 3):
            y_copy(n, slot).start()
        return carry

    lax.fori_loop(0, PIECES, update, 0)

    def relay(n):
        y_copy(n, 1).wait_recv()
        ut[n, pl.ds(right_rows, half), :] += yrecv[n, 1]
        y_copy(n, 2).start()
        y_copy(n, 4).wait_recv()
        ut[n, pl.ds(left_rows + half, half), :] += yrecv[n, 4]
        y_copy(n, 5).start()

    def y_sum(n):
        for slot in (0, 2, 3, 5):
            y_copy(n, slot).wait_recv()
        columns = slice(n % 2 * PIECE, (n % 2 + 1) * PIECE)
        w[n // 2, :half, columns] = ut[n, pl.ds(own_rows, half), :] + (yrecv[n, 2] + yrecv[n, 3])
        w[n // 2, half:, columns] = ut[n, pl.ds(own_rows + half, half), :] + (yrecv[n, 0] + yrecv[n, 5])

    def z_copies(h):
        copies = []
        for d in range(1, NZ):
            target = z_peer(d)
            start = pl.multiple_of(lax.rem(z + d, NZ) * own, own)
            copies.append(
                remote(w.at[h, pl.ds(start, own), :], zrecv.at[h, d - 1], z_s.at[h, d - 1], z_r.at[h, d - 1], target, col)
            )
        return copies

    relay(3)
    relay(2)

    loads[6].wait()
    remote(panel_hbm, lf.at[:, col], pc_s.at[0], pc_r.at[0], row, other).wait_recv()
    at = pl.multiple_of(x * SUB, SUB)
    blk[...] = jnp.concatenate(
        [lf[core, 2 * x, :, pl.ds(at, SUB)], lf[core, 2 * x + 1, :, pl.ds(at, SUB)]], axis=0
    )
    dinv[core, x] = unit_inverse(blk[...])
    mine = dinv.at[core, x]
    for d in range(1, NX):
        remote(mine, mine, dx_s.at[d - 1], dx_r.at[d - 1], row, x_peer(d)).start()
    remote(mine, mine, dc_s.at[0], dc_r.at[0], row, other).start()

    relay(1)
    relay(0)
    for h in (1, 0):
        y_sum(2 * h + 1)
        y_sum(2 * h)
        for copy in z_copies(h):
            copy.start()

    def forward_panel(d):
        shard = lf.at[:, lax.rem(x + NX - d, NX) * 2 + core]
        return remote(shard, shard, pc_s.at[d], pc_r.at[d], row, other)

    def forward_inverse(d):
        inverse = dinv.at[core, lax.rem(x + NX - d, NX)]
        return remote(inverse, inverse, dc_s.at[d], dc_r.at[d], row, other)

    for d in range(1, NX):
        remote(panel_hbm, lf.at[:, col], px_s.at[d - 1], px_r.at[d - 1], row, x_peer(d)).wait_recv()
        forward_panel(d).start()
    for d in range(1, NX):
        remote(mine, mine, dx_s.at[d - 1], dx_r.at[d - 1], row, x_peer(d)).wait_recv()
        forward_inverse(d).start()
    remote(mine, mine, dc_s.at[0], dc_r.at[0], row, other).wait_recv()
    for d in range(1, NX):
        forward_panel(d).wait_recv()
        forward_inverse(d).wait_recv()

    def whole_inverse(m):
        def lower(i, j):
            block = lf[m, :, :, SUB * j : SUB * (j + 1)].reshape(BLOCK, SUB)
            return block[SUB * i : SUB * (i + 1)]

        def pair(i):
            first, second = dinv[m, i], dinv[m, i + 1]
            below = -mm_split(mm_exact(second, lower(i + 1, i)), first)
            top = jnp.concatenate([first, jnp.zeros_like(first)], axis=1)
            return jnp.concatenate([top, jnp.concatenate([below, second], axis=1)], axis=0)

        first, second = pair(0), pair(2)
        off = lf[m, :, :, : 2 * SUB].reshape(BLOCK, 2 * SUB)[2 * SUB :]
        below = -mm_split(mm_exact(second, off), first)
        for rows, columns, value in (
            (slice(0, 2 * SUB), slice(0, 2 * SUB), first),
            (slice(0, 2 * SUB), slice(2 * SUB, BLOCK), jnp.zeros_like(first)),
            (slice(2 * SUB, BLOCK), slice(0, 2 * SUB), below),
            (slice(2 * SUB, BLOCK), slice(2 * SUB, BLOCK), second),
        ):
            high, low = split(value)
            mh[m, rows, columns] = high
            ml[m, rows, columns] = low

    whole_inverse(1)
    whole_inverse(0)

    def reduced(h):
        for copy in z_copies(h):
            copy.wait_recv()
        total = w[h, pl.ds(pl.multiple_of(z * own, own), own), :]
        for d in range(1, NZ):
            total = total + zrecv[h, d - 1]
        return -total

    def solve(h, value):
        high, low = split(value)
        return mm(high, mh[h]) + (mm(low, mh[h]) + mm(high, ml[h]))

    def gz_copies(h):
        mine_rows = g.at[h, pl.ds(pl.multiple_of(row * own, own), own), :]
        return [
            remote(mine_rows, mine_rows, gz_s.at[h, d - 1], gz_r.at[h, d - 1], z_peer(d), col)
            for d in range(1, NZ)
        ]

    def publish(h, value):
        g[h, pl.ds(pl.multiple_of(row * own, own), own), :] = value
        for copy in gz_copies(h):
            copy.start()

    second = solve(1, reduced(1))
    publish(1, second)
    coupling = lf[2].reshape(BLOCK, BLOCK)
    first = solve(0, reduced(0) - mm_exact(second, coupling))
    publish(0, first)

    def gy_copy(h, slot):
        start, size, target = (
            (own_rows, group, right), (own_rows, group, left),
            (left_rows, half, right), (right_rows + half, half, left),
        )[slot]
        rows = g.at[h, pl.ds(start, size), :]
        return remote(rows, rows, gy_s.at[h, slot], gy_r.at[h, slot], target, col)

    for h in (1, 0):
        for copy in gz_copies(h):
            copy.wait_recv()
        gy_copy(h, 0).start()
        gy_copy(h, 1).start()
    for h in (1, 0):
        gy_copy(h, 0).wait_recv()
        gy_copy(h, 2).start()
        gy_copy(h, 1).wait_recv()
        gy_copy(h, 3).start()
    for h in (1, 0):
        gy_copy(h, 2).wait_recv()
        gy_copy(h, 3).wait_recv()
        out_ref[h * BLOCK : (h + 1) * BLOCK, :] = g[h].T

    for n in range(PIECES):
        for slot in range(6):
            y_copy(n, slot).wait_send()
    for h in (1, 0):
        for copy in (*z_copies(h), *gz_copies(h)):
            copy.wait_send()
        for slot in range(4):
            gy_copy(h, slot).wait_send()
    for d in range(1, NX):
        remote(panel_hbm, lf.at[:, col], px_s.at[d - 1], px_r.at[d - 1], row, x_peer(d)).wait_send()
        remote(mine, mine, dx_s.at[d - 1], dx_r.at[d - 1], row, x_peer(d)).wait_send()
        forward_panel(d).wait_send()
        forward_inverse(d).wait_send()
    remote(panel_hbm, lf.at[:, col], pc_s.at[0], pc_r.at[0], row, other).wait_send()
    remote(mine, mine, dc_s.at[0], dc_r.at[0], row, other).wait_send()


def shards(tail_factor, tail_solution, panel_rhs, panel_factor):
    depth, window = tail_factor.shape
    width = tail_solution.shape[1]
    group, own = width // NY, width // (NY * NZ)
    slab = panel_factor.shape[1]
    dma = pltpu.SemaphoreType.DMA
    scratch = [
        pltpu.VMEM((PIECES, depth, PIECE), BF16),
        pltpu.VMEM((depth, width), BF16),
        pltpu.VMEM((width, depth), BF16),
        pltpu.VMEM(panel_rhs.shape, F32),
        pltpu.VMEM((PIECE, width), F32),
        pltpu.VMEM((PIECES, width, PIECE), F32),
        pltpu.VMEM((PIECES, 6, group // 2, PIECE), F32),
        pltpu.VMEM((2, group, BLOCK), F32),
        pltpu.VMEM((2, NZ - 1, own, BLOCK), F32),
        pltpu.VMEM((2, width, BLOCK), F32),
        pltpu.VMEM((3, 2 * NX, slab, BLOCK), BF16),
        pltpu.VMEM((SUB, SUB), BF16),
        pltpu.VMEM((2, SUBS, SUB, SUB), F32),
        pltpu.VMEM((2, BLOCK, BLOCK), BF16),
        pltpu.VMEM((2, BLOCK, BLOCK), BF16),
        dma((7,)),
        dma((PIECES, 6)), dma((PIECES, 6)),
        dma((2, NZ - 1)), dma((2, NZ - 1)),
        dma((2, NZ - 1)), dma((2, NZ - 1)),
        dma((2, 4)), dma((2, 4)),
        dma((NX - 1,)), dma((NX - 1,)),
        dma((NX,)), dma((NX,)),
        dma((NX - 1,)), dma((NX - 1,)),
        dma((NX,)), dma((NX,)),
    ]
    return pl.pallas_call(
        kernel,
        out_shape=jax.ShapeDtypeStruct((window, width), F32),
        in_specs=[pl.BlockSpec(memory_space=pl.ANY)] * 4,
        out_specs=pl.BlockSpec(memory_space=pltpu.VMEM),
        scratch_shapes=scratch,
        compiler_params=pltpu.CompilerParams(
            collective_id=0, has_side_effects=True, vmem_limit_bytes=60 * 1024 * 1024
        ),
    )(tail_factor, tail_solution, panel_rhs, panel_factor)


def solution(mesh):
    return jax.shard_map(
        shards,
        mesh=mesh,
        in_specs=(P("row", None), P("row", "col"), P("row", "col"), P(None, "col", None)),
        out_specs=P(None, "col"),
        check_vma=False,
    )
```

time: 407 us -> 51.5 us (0.13)
  the two profiles are of different devices: /device:TPU:8 before, /device:TPU:1 now
where the time goes in v1:
time: 51.5 us; the launch traced here: 51.4 us
  Pallas kernels  49.1 us (95%)
  local copies, waits for them, and re-layouts  2.26 us (4%)
    pallas_call x1, Pallas kernels, shards(): pl.pallas_call(kernel, out_shape=jax.ShapeDtypeStruct((window, width), F3...  49.1 us
    unnamed x1, local copies, waits for them, and re-layouts  2.26 us

profile of v1, /device:TPU:1, one launch (start us, length us, event | category | flops | bytes accessed | tf_op | source)
XLA Modules:
  0.0 51.4 jit_solution(17352905415890802519)
XLA Ops:
  0.0 49.1 %shard_map.46 = f32[1024,256]{1,0:T(8,128)} custom-call(bf16[4096,1024]{1,0:T(8,128)(2,1)} %a_hbm.1, bf16[4096,256]{1,0:T(8,128)(2,1)} %b_hbm.1, f32[32,256]{1,0:T(8,128)} %rhs_hbm.1, bf16[3,64,512]{2,1,0:T(8,128)(2,1)} %panel_hbm.1), custom_call_target="tpu_custom_call" | custom-call | tf_op jit(solution)/shard_map/pallas_call | solution.py:348
  49.2 2.3 %copy.6 = f32[1024,256]{1,0:T(8,128)} copy(f32[1024,256]{1,0:T(8,128)} %shard_map.46) | data formatting | bytes 2097152

commit v2 on v0

v2 whole, which is shorter than its diff:
```python
import jax
import jax.numpy as jnp
from jax import lax
from jax.experimental import pallas as pl
from jax.experimental.pallas import tpu as pltpu
from jax.sharding import PartitionSpec as P

MESH = pl.DeviceIdType.MESH
F32 = jnp.float32
BF16 = jnp.bfloat16

NY, NZ, NX = 4, 8, 4
BLOCK = 512
WINDOW = 2 * BLOCK
PIECE = 256
PIECES = WINDOW // PIECE
SUB = 128
CHUNKS = 4
NEAR, FAR = (1, 7, 2, 6), (3, 5, 4)
Z_ORDER = (4, 3, 5, 2, 6, 1, 7)
Y_SLOT = (2, 0, 3, 4, 1, 5)
Y_SEM = (2, 0, 2, 2, 1, 2)
PARTS = 4


def split(x):
    high = x.astype(BF16)
    return high, (x - high.astype(F32)).astype(BF16)


def mm(a, b):
    return jnp.dot(a, b, preferred_element_type=F32)


def mm_exact(a, b):
    high, low = split(a)
    return mm(high, b) + mm(low, b)


def mm_split(a, b):
    a_high, a_low = split(a)
    b_high, b_low = split(b)
    return mm(a_high, b_high) + (mm(a_low, b_high) + mm(a_high, b_low))


def stacked(a, b):
    rows = a.shape[0]
    both = mm(jnp.concatenate(split(a), axis=0), b)
    return both[:rows] + both[rows:]


def within(size):
    row = lax.broadcasted_iota(jnp.int32, (SUB, SUB), 0)
    col = lax.broadcasted_iota(jnp.int32, (SUB, SUB), 1)
    return (row // (2 * size) == col // (2 * size)) & (row // size == col // size + 1)


def unit_inverse(block):
    row = lax.broadcasted_iota(jnp.int32, (SUB, SUB), 0)
    col = lax.broadcasted_iota(jnp.int32, (SUB, SUB), 1)
    inverse = jnp.where(row == col, 1.0, 0.0) - jnp.where(within(1), block, 0.0)
    size = 2
    while size < SUB // 2:
        below = jnp.where(within(size), block, 0.0).astype(BF16)
        inverse = inverse - mm_split(mm_exact(inverse, below), inverse)
        size *= 2
    return inverse


def kernel(
    a_hbm, b_hbm, rhs_hbm, panel_hbm, out_ref,
    a_v, b_v, bt, rhs_v, place, ut, yrecv, w, zrecv, g, lf, dall, mh, ml,
    load_b, load_a, load_s, y_s, y_r, z_s, z_r, gz_s, gz_r, gy_s, gy_r, px_s, px_r, pc_s, pc_r,
):
    row, col = lax.axis_index("row"), lax.axis_index("col")
    y, z = row // NZ, row % NZ
    x, core = col // 2, col % 2
    other = x * 2 + (1 - core)
    right = lax.rem(y + 1, NY) * NZ + z
    left = lax.rem(y + NY - 1, NY) * NZ + z
    depth, width = b_hbm.shape
    group = width // NY
    half = group // 2
    own = width // (NY * NZ)
    slab = panel_hbm.shape[1]

    def remote(src, dst, send, recv, r, c):
        return pltpu.make_async_remote_copy(
            src_ref=src, dst_ref=dst, send_sem=send, recv_sem=recv,
            device_id=(r, c), device_id_type=MESH,
        )

    def z_peer(d):
        return y * NZ + lax.rem(z + d, NZ)

    def y_peer(d):
        return lax.rem(y + d, NY) * NZ + z

    def z_rows(start, d):
        return pl.ds(pl.multiple_of(start + lax.rem(z + d, NZ) * own, own), own)

    def all_sent(sem, ref):
        remote(ref, ref, sem, sem, row, col).wait_send()

    def all_here(sem, ref):
        remote(ref, ref, sem, sem, row, col).wait_recv()

    def x_peer(d):
        return lax.rem(x + d, NX) * 2 + core

    barrier = pltpu.get_barrier_semaphore()

    def greet(r, c):
        pl.semaphore_signal(barrier, inc=1, device_id=(r, c), device_id_type=MESH)

    for d in Z_ORDER:
        greet(z_peer(d), col)
    for d in (2, 1, 3):
        greet(row, x_peer(d))
    for d in range(1, NY):
        greet(y_peer(d), col)
    greet(row, other)

    chunk = depth // CHUNKS
    load_panel = pltpu.make_async_copy(panel_hbm, lf.at[:, col], load_s.at[0])
    load_rhs = pltpu.make_async_copy(rhs_hbm, rhs_v, load_s.at[1])
    loads_b = [
        pltpu.make_async_copy(
            b_hbm.at[chunk * k : chunk * (k + 1), :], b_v.at[chunk * k : chunk * (k + 1), :], load_b.at[k]
        )
        for k in range(CHUNKS)
    ]

    def load(n):
        return pltpu.make_async_copy(a_hbm.at[:, PIECE * n : PIECE * (n + 1)], a_v.at[n], load_a.at[n])

    load_panel.start()
    for copy in loads_b:
        copy.start()
    load(3).start()
    load_rhs.start()

    load_panel.wait()
    at = pl.multiple_of(x * SUB, SUB)
    tiles = [lf[m, col, :, pl.ds(at, SUB)].astype(F32) for m in (0, 1)]
    turned = [pltpu.roll(tile, slab, 1) for tile in tiles]
    even = core == 0
    block = jnp.concatenate([jnp.where(even, tiles[0], turned[0]), jnp.where(even, turned[1], tiles[1])], axis=0)
    inverse = unit_inverse(block)
    dall[col] = inverse[:slab] + inverse[slab:]

    for k in range(CHUNKS):
        loads_b[k].wait()
        bt[:, chunk * k : chunk * (k + 1)] = b_v[chunk * k : chunk * (k + 1), :].T

    load(2).start()

    pl.semaphore_wait(barrier, (NY - 1) + (NZ - 1) + (NX - 1) + 1)

    def part(p, c):
        return dall.at[c] if p == 0 else lf.at[(1, 0, 2)[p - 1], c]

    def along_x(p, d):
        return remote(part(p, col), part(p, col), px_s.at[p], px_r.at[p, d - 1], row, x_peer(d))

    def across(p, d):
        shard = part(p, lax.rem(x + NX - d, NX) * 2 + core)
        return remote(shard, shard, pc_s.at[p], pc_r.at[p], row, other)

    def send_panel(p):
        for d in (2, 1, 3):
            along_x(p, d).start()
        across(p, 0).start()

    send_panel(0)
    send_panel(1)

    place[...] = jnp.zeros_like(place)
    load_rhs.wait()
    place[pl.ds(pl.multiple_of(z * (PIECE // NZ), 8), PIECE // NZ), :] = rhs_v[...]

    def y_group(target):
        return pl.multiple_of(target // NZ * group, group)

    right_rows, left_rows = y_group(right), y_group(left)
    far_rows = pl.multiple_of(lax.rem(y + 2, NY) * group, group)
    own_rows = pl.multiple_of(y * group, group)

    def y_copy(n, slot):
        start = ((right_rows, 1), (far_rows, 0), (right_rows, 0), (left_rows, 0), (far_rows, 1), (left_rows, 1))[slot]
        src = ut.at[n, pl.ds(start[0] + start[1] * half, half), :]
        target = right if slot < 3 else left
        return remote(src, yrecv.at[n, Y_SLOT[slot]], y_s, y_r.at[n, Y_SEM[slot]], target, col)

    def y_start(n, slots):
        for slot in slots:
            y_copy(n, slot).start()

    def update(n):
        load(n).wait()
        if n >= 2:
            load(n - 2).start()
        ut[n] = mm(bt[...], a_v[n])

        @pl.when(n == y)
        def _():
            ut[n] = ut[n] - place[...].T

    def relay(n):
        all_here(y_r.at[n, 0], yrecv.at[n, 0])
        ut[n, pl.ds(right_rows, half), :] += yrecv[n, 0]
        y_copy(n, 2).start()
        all_here(y_r.at[n, 1], yrecv.at[n, 1])
        ut[n, pl.ds(left_rows + half, half), :] += yrecv[n, 1]
        y_copy(n, 5).start()

    def z_copy(n, d):
        return remote(w.at[n, z_rows(0, d), :], zrecv.at[n, d - 1], z_s, z_r.at[n], z_peer(d), col)

    def y_sum(n):
        all_here(y_r.at[n, 2], yrecv.at[n, 2:6])
        w[n, :half, :] = ut[n, pl.ds(own_rows, half), :] + (yrecv[n, 3] + yrecv[n, 4])
        w[n, half:, :] = ut[n, pl.ds(own_rows + half, half), :] + (yrecv[n, 2] + yrecv[n, 5])
        for d in Z_ORDER:
            z_copy(n, d).start()

    def forward(p):
        for d in range(1, NX):
            along_x(p, d).wait_recv()
            across(p, d).start()

    def arrived(p):
        all_here(pc_r.at[p], dall.at[0:NX] if p == 0 else lf.at[0, 0:NX])

    update(3)
    y_start(3, (1, 4))
    update(2)
    y_start(2, (1, 4))
    y_start(3, (0, 3))
    update(1)
    y_start(1, (1, 4))
    relay(3)
    y_start(2, (0, 3))
    update(0)
    y_start(0, (1, 4))
    relay(2)
    y_start(1, (0, 3))
    send_panel(2)
    relay(1)
    y_start(0, (0, 3))
    forward(0)
    forward(1)
    y_sum(3)
    relay(0)
    send_panel(3)
    y_sum(2)
    y_sum(1)

    def whole_inverse(m):
        lane = lax.broadcasted_iota(jnp.int32, (slab, SUB), 1)

        def small(i):
            first, second = dall[2 * i], dall[2 * i + 1]
            if m == 0:
                second = pltpu.roll(second, slab, 1)
            else:
                first = pltpu.roll(first, slab, 1)
            first = jnp.where(lane < slab, first, 0.0)
            second = jnp.where(lane < slab, 0.0, second)
            value = jnp.concatenate([first, second], axis=0)
            diagonal = lower(i, i)
            below = jnp.where(within(slab), diagonal, jnp.zeros_like(diagonal))
            return value - mm_split(mm_exact(value, below), value)

        def lower(i, j):
            return lf[m, 2 * i : 2 * i + 2, :, SUB * j : SUB * (j + 1)].reshape(SUB, SUB)

        def pair(i):
            first, second = small(i), small(i + 1)
            below = -mm_split(mm_exact(second, lower(i + 1, i)), first)
            top = jnp.concatenate([first, jnp.zeros_like(first)], axis=1)
            return jnp.concatenate([top, jnp.concatenate([below, second], axis=1)], axis=0)

        first, second = pair(0), pair(2)
        off = lf[m, 4:, :, : 2 * SUB].reshape(2 * SUB, 2 * SUB)
        below = -mm_split(mm_exact(second, off), first)
        for rows, columns, value in (
            (slice(0, 2 * SUB), slice(0, 2 * SUB), first),
            (slice(0, 2 * SUB), slice(2 * SUB, BLOCK), jnp.zeros_like(first)),
            (slice(2 * SUB, BLOCK), slice(0, 2 * SUB), below),
            (slice(2 * SUB, BLOCK), slice(2 * SUB, BLOCK), second),
        ):
            high, low = split(value)
            mh[m, rows, columns] = high
            ml[m, rows, columns] = low

    def reduced(h):
        pieces = []
        for n in (2 * h, 2 * h + 1):
            all_here(z_r.at[n], zrecv.at[n])
            total = w[n, z_rows(0, 0), :]
            for d in range(1, NZ):
                total = total + zrecv[n, d - 1]
            pieces.append(-total)
        return jnp.concatenate(pieces, axis=1)

    def solve(h, value):
        return stacked(value, mh[h]) + mm(value.astype(BF16), ml[h])

    def gz_copy(h, d):
        rows = g.at[h, z_rows(own_rows, 0), :]
        return remote(rows, rows, gz_s, gz_r.at[h, 0 if d in NEAR else 1], z_peer(d), col)

    def spread(h, distances):
        for d in distances:
            rows = g.at[h, z_rows(own_rows, d), :]
            for side in (2, 1, 3):
                remote(rows, rows, gy_s, gy_r.at[h], y_peer(side), col).start()

    def publish(h, value):
        g[h, z_rows(own_rows, 0), :] = value
        for d in Z_ORDER:
            gz_copy(h, d).start()
        spread(h, (0,))

    def spread_near(h):
        all_here(gz_r.at[h, 0], g.at[h, 0 : 4 * own, :])
        spread(h, NEAR)

    def spread_far(h):
        all_here(gz_r.at[h, 1], g.at[h, 0 : 3 * own, :])
        spread(h, FAR)

    def finish(h):
        all_here(gy_r.at[h], g.at[h, 0 : 3 * group, :])
        out_ref[h * BLOCK : (h + 1) * BLOCK, :] = g[h].T

    arrived(0)
    arrived(1)
    whole_inverse(1)
    y_sum(0)
    forward(2)
    second = solve(1, reduced(1))
    publish(1, second)
    forward(3)
    arrived(2)
    whole_inverse(0)
    arrived(3)
    coupled = stacked(second, lf[2].reshape(BLOCK, BLOCK))
    first = solve(0, reduced(0) - coupled)
    publish(0, first)
    spread_near(1)
    spread_far(1)
    spread_near(0)
    spread_far(0)
    all_sent(y_s, yrecv)
    all_sent(z_s, zrecv)
    for p in range(PARTS):
        across_size = dall.at[0:NX] if p == 0 else lf.at[0, 0:NX]
        along_size = dall.at[0 : NX - 1] if p == 0 else lf.at[0, 0 : NX - 1]
        all_sent(px_s.at[p], along_size)
        all_sent(pc_s.at[p], across_size)
    finish(1)
    all_sent(gz_s, g.at[:, 0 : 7 * own, :])
    finish(0)
    all_sent(gy_s, g.at[:, 0 : 3 * group, :])


def shards(tail_factor, tail_solution, panel_rhs, panel_factor):
    depth, window = tail_factor.shape
    width = tail_solution.shape[1]
    group, own = width // NY, width // (NY * NZ)
    slab = panel_factor.shape[1]
    dma = pltpu.SemaphoreType.DMA
    scratch = [
        pltpu.VMEM((PIECES, depth, PIECE), BF16),
        pltpu.VMEM((depth, width), BF16),
        pltpu.VMEM((width, depth), BF16),
        pltpu.VMEM(panel_rhs.shape, F32),
        pltpu.VMEM((PIECE, width), F32),
        pltpu.VMEM((PIECES, width, PIECE), F32),
        pltpu.VMEM((PIECES, 6, group // 2, PIECE), F32),
        pltpu.VMEM((PIECES, group, PIECE), F32),
        pltpu.VMEM((PIECES, NZ - 1, own, PIECE), F32),
        pltpu.VMEM((2, width, BLOCK), F32),
        pltpu.VMEM((3, 2 * NX, slab, BLOCK), BF16),
        pltpu.VMEM((2 * NX, slab, SUB), F32),
        pltpu.VMEM((2, BLOCK, BLOCK), BF16),
        pltpu.VMEM((2, BLOCK, BLOCK), BF16),
        dma((CHUNKS,)), dma((PIECES,)), dma((2,)),
        dma, dma((PIECES, 3)),
        dma, dma((PIECES,)),
        dma, dma((2, 2)),
        dma, dma((2,)),
        dma((PARTS,)), dma((PARTS, NX - 1)),
        dma((PARTS,)), dma((PARTS,)),
    ]
    return pl.pallas_call(
        kernel,
        out_shape=jax.ShapeDtypeStruct((window, width), F32),
        in_specs=[pl.BlockSpec(memory_space=pltpu.HBM)] * 4,
        out_specs=pl.BlockSpec(memory_space=pltpu.VMEM),
        scratch_shapes=scratch,
        compiler_params=pltpu.CompilerParams(
            collective_id=0, has_side_effects=True, vmem_limit_bytes=60 * 1024 * 1024
        ),
    )(tail_factor, tail_solution, panel_rhs, panel_factor)


def solution(mesh):
    return jax.shard_map(
        shards,
        mesh=mesh,
        in_specs=(P("row", None), P("row", "col"), P("row", "col"), P(None, "col", None)),
        out_specs=P(None, "col"),
        check_vma=False,
    )
```

time: 407 us -> 44.7 us (0.11)
  waiting for transfers between devices: 254 us -> 0 us
  other arithmetic: 87 us -> 0 us
  Pallas kernels: 0 us -> 41.6 us
  local copies, waits for them, and re-layouts: 28.6 us -> 2.26 us
  matrix products: 21.6 us -> 0 us
  between operations: 13.3 us -> 0.01 us
    psum x1 -> x0, waiting for transfers between devices: 151 us -> none  [shards(): summed = lax.psum(term, 'row')]
    all_gather x2 -> x0, waiting for transfers between devices: 102 us -> none  [the longest x1 76.4 us: shards(): whole_rhs = lax.all_gather(panel_rhs, 'row', axis=0, tiled=True)]
    another operation x5 -> x0, other arithmetic: 82.4 us -> none  [solve_block(): jax.scipy.linalg.solve_triangular(lower, rhs, trans=1, lower=True, unit_d...]
    pallas_call x0 -> x1, Pallas kernels: none -> 41.6 us  [shards(): pl.pallas_call(kernel, out_shape=jax.ShapeDtypeStruct((window, width), F3...]
    another operation x27 -> x0, local copies, waits for them, and re-layouts: 25.8 us -> none  [solve_block(): jax.scipy.linalg.solve_triangular(lower, rhs, trans=1, lower=True, unit_d...]
    another operation x14 -> x0, matrix products: 13 us -> none  [solve_block(): jax.scipy.linalg.solve_triangular(lower, rhs, trans=1, lower=True, unit_d...]
    dot_general x2 -> x0, matrix products: 8.59 us -> none  [the longest x1 6.71 us: local_update(): lax.dot_general(tail_factor, tail_solution, (((0,), (0,)), ((), ())), pre...]
  transfers between devices with their start and end apart: 3 -> 0, of which waited for: 3 -> 0; matrix products, arithmetic and copies ran while one was open for 0% -> 0% of each run, Pallas kernels for 0% -> 0%
where the time goes in v2:
time: 44.7 us; the launch traced here: 43.9 us
  Pallas kernels  41.6 us (93%)
  local copies, waits for them, and re-layouts  2.26 us (5%)
    pallas_call x1, Pallas kernels, shards(): pl.pallas_call(kernel, out_shape=jax.ShapeDtypeStruct((window, width), F3...  41.6 us
    unnamed x1, local copies, waits for them, and re-layouts  2.26 us

profile of v2, /device:TPU:8, one launch (start us, length us, event | category | flops | bytes accessed | tf_op | source)
XLA Modules:
  0.0 43.9 jit_solution(12383284607432935511)
XLA Ops:
  0.0 41.6 %shard_map.46 = f32[1024,256]{1,0:T(8,128)} custom-call(bf16[4096,1024]{1,0:T(8,128)(2,1)} %a_hbm.1, bf16[4096,256]{1,0:T(8,128)(2,1)} %b_hbm.1, f32[32,256]{1,0:T(8,128)} %rhs_hbm.1, bf16[3,64,512]{2,1,0:T(8,128)(2,1)} %panel_hbm.1), custom_call_target="tpu_custom_call" | custom-call | tf_op jit(solution)/shard_map/pallas_call | solution.py:398
  41.6 2.3 %copy.6 = f32[1024,256]{1,0:T(8,128)} copy(f32[1024,256]{1,0:T(8,128)} %shard_map.46) | data formatting | bytes 2097152

commit v3 on v2

--- a/solution.py
+++ b/solution.py
@@ -18,6 +18,7 @@
 CHUNKS = 4
 NEAR, FAR = (1, 7, 2, 6), (3, 5, 4)
 Z_ORDER = (4, 3, 5, 2, 6, 1, 7)
+WHOLE, FRONT, BACK = slice(0, BLOCK), slice(0, BLOCK // 2), slice(BLOCK // 2, BLOCK)
 Y_SLOT = (2, 0, 3, 4, 1, 5)
 Y_SEM = (2, 0, 2, 2, 1, 2)
 PARTS = 4
@@ -255,6 +256,7 @@
     send_panel(3)
     y_sum(2)
     y_sum(1)
+    forward(2)
 
     def whole_inverse(m):
         lane = lax.broadcasted_iota(jnp.int32, (slab, SUB), 1)
@@ -311,48 +313,69 @@
         rows = g.at[h, z_rows(own_rows, 0), :]
         return remote(rows, rows, gz_s, gz_r.at[h, 0 if d in NEAR else 1], z_peer(d), col)
 
-    def spread(h, distances):
+    def gy_copy(h, d, start, columns, sem, side):
+        rows = g.at[h, z_rows(start, d), columns]
+        return remote(rows, rows, gy_s, gy_r.at[h, sem], y_peer(side), col)
+
+    def spread(h, distances, wave):
         for d in distances:
-            rows = g.at[h, z_rows(own_rows, d), :]
-            for side in (2, 1, 3):
-                remote(rows, rows, gy_s, gy_r.at[h], y_peer(side), col).start()
+            gy_copy(h, d, own_rows, WHOLE, wave, 1).start()
+            gy_copy(h, d, own_rows, WHOLE, 3 + wave, 3).start()
+
+    def pass_on(h, distances, wave):
+        size = g.at[h, 0 : len(distances) * own, :]
+        all_here(gy_r.at[h, wave], size)
+        for d in distances:
+            gy_copy(h, d, left_rows, FRONT, 6, 1).start()
+        all_here(gy_r.at[h, 3 + wave], size)
+        for d in distances:
+            gy_copy(h, d, right_rows, BACK, 6, 3).start()
 
     def publish(h, value):
         g[h, z_rows(own_rows, 0), :] = value
         for d in Z_ORDER:
             gz_copy(h, d).start()
-        spread(h, (0,))
+        spread(h, (0,), 0)
 
     def spread_near(h):
         all_here(gz_r.at[h, 0], g.at[h, 0 : 4 * own, :])
-        spread(h, NEAR)
+        spread(h, NEAR, 1)
 
     def spread_far(h):
         all_here(gz_r.at[h, 1], g.at[h, 0 : 3 * own, :])
-        spread(h, FAR)
+        if h == 0:
+            for d in FAR:
+                gy_copy(h, d, own_rows, WHOLE, 6, 2).start()
+        spread(h, FAR, 2)
 
     def finish(h):
-        all_here(gy_r.at[h], g.at[h, 0 : 3 * group, :])
+        if h == 0:
+            all_here(gy_r.at[h, 2], g.at[h, 0 : 3 * own, :])
+            all_here(gy_r.at[h, 5], g.at[h, 0 : 3 * own, :])
+        all_here(gy_r.at[h, 6], g.at[h, 0:group, :])
         out_ref[h * BLOCK : (h + 1) * BLOCK, :] = g[h].T
 
     arrived(0)
     arrived(1)
     whole_inverse(1)
     y_sum(0)
-    forward(2)
-    second = solve(1, reduced(1))
-    publish(1, second)
     forward(3)
     arrived(2)
     whole_inverse(0)
+    second = solve(1, reduced(1))
+    publish(1, second)
     arrived(3)
     coupled = stacked(second, lf[2].reshape(BLOCK, BLOCK))
     first = solve(0, reduced(0) - coupled)
     publish(0, first)
+    pass_on(1, (0,), 0)
     spread_near(1)
     spread_far(1)
     spread_near(0)
+    pass_on(1, NEAR, 1)
+    pass_on(0, (0,), 0)
     spread_far(0)
+    pass_on(1, FAR, 2)
     all_sent(y_s, yrecv)
     all_sent(z_s, zrecv)
     for p in range(PARTS):
@@ -360,6 +383,7 @@
         along_size = dall.at[0 : NX - 1] if p == 0 else lf.at[0, 0 : NX - 1]
         all_sent(px_s.at[p], along_size)
         all_sent(pc_s.at[p], across_size)
+    pass_on(0, NEAR, 1)
     finish(1)
     all_sent(gz_s, g.at[:, 0 : 7 * own, :])
     finish(0)
@@ -391,7 +415,7 @@
         dma, dma((PIECES, 3)),
         dma, dma((PIECES,)),
         dma, dma((2, 2)),
-        dma, dma((2,)),
+        dma, dma((2, 7)),
         dma((PARTS,)), dma((PARTS, NX - 1)),
         dma((PARTS,)), dma((PARTS,)),
     ]
@@ -402,7 +426,7 @@
         out_specs=pl.BlockSpec(memory_space=pltpu.VMEM),
         scratch_shapes=scratch,
         compiler_params=pltpu.CompilerParams(
-            collective_id=0, has_side_effects=True, vmem_limit_bytes=60 * 1024 * 1024
+            collective_id=0, has_side_effects=True, vmem_limit_bytes=52 * 1024 * 1024
         ),
     )(tail_factor, tail_solution, panel_rhs, panel_factor)
 

time: 44.7 us -> 44 us (0.984); the launches traced: 43.9 us -> 43.6 us
  Pallas kernels: 41.6 us -> 41 us
    pallas_call x1, Pallas kernels: 41.6 us -> 41 us  [shards(): pl.pallas_call(kernel, out_shape=jax.ShapeDtypeStruct((window, width), F3...]
    unnamed x1 -> x5, local copies, waits for them, and re-layouts: 2.26 us -> 2.66 us
where the time goes in v3:
time: 44 us; the launch traced here: 43.6 us
  Pallas kernels  41 us (93%)
  local copies, waits for them, and re-layouts  2.66 us (6%)
    pallas_call x1, Pallas kernels, shards(): pl.pallas_call(kernel, out_shape=jax.ShapeDtypeStruct((window, width), F3...  41 us
    unnamed x5, local copies, waits for them, and re-layouts  2.66 us

profile of v3, /device:TPU:8, one launch (start us, length us, event | category | flops | bytes accessed | tf_op | source)
XLA Modules:
  0.0 43.6 jit_solution(14742058338163771059)
XLA Ops:
  0.0 0.0 copy-start
  0.0 0.9 %copy-done = bf16[3,64,512]{2,1,0:T(8,128)(2,1)S(1)} copy-done((bf16[3,64,512]{2,1,0:T(8,128)(2,1)S(1)}, bf16[3,64,512]{2,1,0:T(8,128)(2,1)}, u32[]{:S(2)}) %copy-start) | copy-done | bytes 196632
  0.9 0.0 copy-start.1
  0.9 0.8 %copy-done.1 = f32[32,256]{1,0:T(8,128)S(1)} copy-done((f32[32,256]{1,0:T(8,128)S(1)}, f32[32,256]{1,0:T(8,128)}, u32[]{:S(2)}) %copy-start.1) | copy-done | bytes 32792
  1.7 41.0 %shard_map.46 = f32[1024,256]{1,0:T(8,128)S(1)} custom-call(bf16[4096,1024]{1,0:T(8,128)(2,1)} %a_hbm.1, bf16[4096,256]{1,0:T(8,128)(2,1)} %b_hbm.1, f32[32,256]{1,0:T(8,128)S(1)} %copy-done.1, bf16[3,64,512]{2,1,0:T(8,128)(2,1)S(1)} %copy-done), custom_call_target="tpu_custom_call" | custom-call | tf_op jit(solution)/shard_map/pallas_call | solution.py:422
  42.7 1.0 %copy.6 = f32[1024,256]{1,0:T(8,128)} copy(f32[1024,256]{1,0:T(8,128)S(1)} %shard_map.46) | data formatting | bytes 2097152
Async XLA Ops:
  0.0 0.9 %copy-start = (bf16[3,64,512]{2,1,0:T(8,128)(2,1)S(1)}, bf16[3,64,512]{2,1,0:T(8,128)(2,1)}, u32[]{:S(2)}) copy-start(bf16[3,64,512]{2,1,0:T(8,128)(2,1)} %panel_hbm.1) | copy-start | bytes 589828
  0.9 0.8 %copy-start.1 = (f32[32,256]{1,0:T(8,128)S(1)}, f32[32,256]{1,0:T(8,128)}, u32[]{:S(2)}) copy-start(f32[32,256]{1,0:T(8,128)} %rhs_hbm.1) | copy-start | bytes 98308

commit v4 on v3

--- a/solution.py
+++ b/solution.py
@@ -256,7 +256,6 @@
     send_panel(3)
     y_sum(2)
     y_sum(1)
-    forward(2)
 
     def whole_inverse(m):
         lane = lax.broadcasted_iota(jnp.int32, (slab, SUB), 1)
@@ -359,11 +358,12 @@
     arrived(1)
     whole_inverse(1)
     y_sum(0)
+    forward(2)
+    second = solve(1, reduced(1))
+    publish(1, second)
     forward(3)
     arrived(2)
     whole_inverse(0)
-    second = solve(1, reduced(1))
-    publish(1, second)
     arrived(3)
     coupled = stacked(second, lf[2].reshape(BLOCK, BLOCK))
     first = solve(0, reduced(0) - coupled)

time: 44 us -> 42.6 us (0.968)
  Pallas kernels: 41 us -> 39.8 us
    pallas_call x1, Pallas kernels: 41 us -> 39.8 us  [shards(): pl.pallas_call(kernel, out_shape=jax.ShapeDtypeStruct((window, width), F3...]
where the time goes in v4:
time: 42.6 us; the launch traced here: 42.4 us
  Pallas kernels  39.8 us (93%)
  local copies, waits for them, and re-layouts  2.66 us (6%)
    pallas_call x1, Pallas kernels, shards(): pl.pallas_call(kernel, out_shape=jax.ShapeDtypeStruct((window, width), F3...  39.8 us
    unnamed x5, local copies, waits for them, and re-layouts  2.66 us

profile of v4, /device:TPU:8, one launch (start us, length us, event | category | flops | bytes accessed | tf_op | source)
XLA Modules:
  0.0 42.4 jit_solution(16767369073645415529)
XLA Ops:
  0.0 0.0 copy-start
  0.0 0.9 %copy-done = bf16[3,64,512]{2,1,0:T(8,128)(2,1)S(1)} copy-done((bf16[3,64,512]{2,1,0:T(8,128)(2,1)S(1)}, bf16[3,64,512]{2,1,0:T(8,128)(2,1)}, u32[]{:S(2)}) %copy-start) | copy-done | bytes 196632
  0.9 0.0 copy-start.1
  0.9 0.8 %copy-done.1 = f32[32,256]{1,0:T(8,128)S(1)} copy-done((f32[32,256]{1,0:T(8,128)S(1)}, f32[32,256]{1,0:T(8,128)}, u32[]{:S(2)}) %copy-start.1) | copy-done | bytes 32792
  1.7 39.8 %shard_map.46 = f32[1024,256]{1,0:T(8,128)S(1)} custom-call(bf16[4096,1024]{1,0:T(8,128)(2,1)} %a_hbm.1, bf16[4096,256]{1,0:T(8,128)(2,1)} %b_hbm.1, f32[32,256]{1,0:T(8,128)S(1)} %copy-done.1, bf16[3,64,512]{2,1,0:T(8,128)(2,1)S(1)} %copy-done), custom_call_target="tpu_custom_call" | custom-call | tf_op jit(solution)/shard_map/pallas_call | solution.py:422
  41.5 1.0 %copy.6 = f32[1024,256]{1,0:T(8,128)} copy(f32[1024,256]{1,0:T(8,128)S(1)} %shard_map.46) | data formatting | bytes 2097152
Async XLA Ops:
  0.0 0.9 %copy-start = (bf16[3,64,512]{2,1,0:T(8,128)(2,1)S(1)}, bf16[3,64,512]{2,1,0:T(8,128)(2,1)}, u32[]{:S(2)}) copy-start(bf16[3,64,512]{2,1,0:T(8,128)(2,1)} %panel_hbm.1) | copy-start | bytes 589828
  0.9 0.8 %copy-start.1 = (f32[32,256]{1,0:T(8,128)S(1)}, f32[32,256]{1,0:T(8,128)}, u32[]{:S(2)}) copy-start(f32[32,256]{1,0:T(8,128)} %rhs_hbm.1) | copy-start | bytes 98308

commit v5 on v4

--- a/solution.py
+++ b/solution.py
@@ -428,7 +428,7 @@
         compiler_params=pltpu.CompilerParams(
             collective_id=0, has_side_effects=True, vmem_limit_bytes=52 * 1024 * 1024
         ),
-    )(tail_factor, tail_solution, panel_rhs, panel_factor)
+    )(tail_factor, tail_solution, pltpu.with_memory_space_constraint(panel_rhs, pltpu.HBM), pltpu.with_memory_space_constraint(panel_factor, pltpu.HBM))
 
 
 def solution(mesh):

time: 42.6 us -> 41.4 us (0.972)
  local copies, waits for them, and re-layouts: 2.66 us -> 0.97 us
  Pallas kernels: 39.8 us -> 40.3 us
    unnamed x5 -> x1, local copies, waits for them, and re-layouts: 2.66 us -> 0.97 us
    pallas_call x1, Pallas kernels: 39.8 us -> 40.3 us  [shards(): pl.pallas_call(kernel, out_shape=jax.ShapeDtypeStruct((window, width), F3...]
where the time goes in v5:
time: 41.4 us; the launch traced here: 41.3 us
  Pallas kernels  40.3 us (97%)
  local copies, waits for them, and re-layouts  0.97 us (2%)
    pallas_call x1, Pallas kernels, shards(): pl.pallas_call(kernel, out_shape=jax.ShapeDtypeStruct((window, width), F3...  40.3 us
    unnamed x1, local copies, waits for them, and re-layouts  0.97 us

profile of v5, /device:TPU:8, one launch (start us, length us, event | category | flops | bytes accessed | tf_op | source)
XLA Modules:
  0.0 41.3 jit_solution(3887859460844850992)
XLA Ops:
  0.0 40.3 %shard_map.46 = f32[1024,256]{1,0:T(8,128)S(1)} custom-call(bf16[4096,1024]{1,0:T(8,128)(2,1)} %a_hbm.1, bf16[4096,256]{1,0:T(8,128)(2,1)} %b_hbm.1, f32[32,256]{1,0:T(8,128)} %rhs_hbm.1, bf16[3,64,512]{2,1,0:T(8,128)(2,1)} %panel_hbm.1), custom_call_target="tpu_custom_call" | custom-call | tf_op jit(solution)/shard_map/pallas_call | solution.py:422
  40.3 1.0 %copy.6 = f32[1024,256]{1,0:T(8,128)} copy(f32[1024,256]{1,0:T(8,128)S(1)} %shard_map.46) | data formatting | bytes 2097152

commit v6 on v5

--- a/solution.py
+++ b/solution.py
@@ -135,13 +135,101 @@
     def load(n):
         return pltpu.make_async_copy(a_hbm.at[:, PIECE * n : PIECE * (n + 1)], a_v.at[n], load_a.at[n])
 
-    load_panel.start()
+    load_rhs.start()
     for copy in loads_b:
         copy.start()
     load(3).start()
-    load_rhs.start()
-
+    load_panel.start()
+
+    for k in range(CHUNKS):
+        loads_b[k].wait()
+        bt[:, chunk * k : chunk * (k + 1)] = b_v[chunk * k : chunk * (k + 1), :].T
+
+    load(2).start()
+
+
+    def part(p, c):
+        return dall.at[c] if p == 0 else lf.at[(1, 0, 2)[p - 1], c]
+
+    def along_x(p, d):
+        return remote(part(p, col), part(p, col), px_s.at[p], px_r.at[p, d - 1], row, x_peer(d))
+
+    def across(p, d):
+        shard = part(p, lax.rem(x + NX - d, NX) * 2 + core)
+        return remote(shard, shard, pc_s.at[p], pc_r.at[p], row, other)
+
+    def send_panel(p):
+        for d in (2, 1, 3):
+            along_x(p, d).start()
+        across(p, 0).start()
+
+    place[...] = jnp.zeros_like(place)
+    load_rhs.wait()
+    place[pl.ds(pl.multiple_of(z * (PIECE // NZ), 8), PIECE // NZ), :] = rhs_v[...]
+
+    def y_group(target):
+        return pl.multiple_of(target // NZ * group, group)
+
+    right_rows, left_rows = y_group(right), y_group(left)
+    far_rows = pl.multiple_of(lax.rem(y + 2, NY) * group, group)
+    own_rows = pl.multiple_of(y * group, group)
+
+    def y_copy(n, slot):
+        start = ((right_rows, 1), (far_rows, 0), (right_rows, 0), (left_rows, 0), (far_rows, 1), (left_rows, 1))[slot]
+        src = ut.at[n, pl.ds(start[0] + start[1] * half, half), :]
+        target = right if slot < 3 else left
+        return remote(src, yrecv.at[n, Y_SLOT[slot]], y_s, y_r.at[n, Y_SEM[slot]], target, col)
+
+    def y_start(n, slots):
+        for slot in slots:
+            y_copy(n, slot).start()
+
+    def update(n):
+        load(n).wait()
+        if n >= 2:
+            load(n - 2).start()
+        ut[n] = mm(bt[...], a_v[n])
+
+        @pl.when(n == y)
+        def _():
+            ut[n] = ut[n] - place[...].T
+
+    def relay(n):
+        all_here(y_r.at[n, 0], yrecv.at[n, 0])
+        ut[n, pl.ds(right_rows, half), :] += yrecv[n, 0]
+        y_copy(n, 2).start()
+        all_here(y_r.at[n, 1], yrecv.at[n, 1])
+        ut[n, pl.ds(left_rows + half, half), :] += yrecv[n, 1]
+        y_copy(n, 5).start()
+
+    def z_copy(n, d):
+        return remote(w.at[n, z_rows(0, d), :], zrecv.at[n, d - 1], z_s, z_r.at[n], z_peer(d), col)
+
+    def y_sum(n):
+        all_here(y_r.at[n, 2], yrecv.at[n, 2:6])
+        w[n, :half, :] = ut[n, pl.ds(own_rows, half), :] + (yrecv[n, 3] + yrecv[n, 4])
+        w[n, half:, :] = ut[n, pl.ds(own_rows + half, half), :] + (yrecv[n, 2] + yrecv[n, 5])
+        for d in Z_ORDER:
+            z_copy(n, d).start()
+
+    def forward(p):
+        for d in range(1, NX):
+            along_x(p, d).wait_recv()
+            across(p, d).start()
+
+    def arrived(p):
+        all_here(pc_r.at[p], dall.at[0:NX] if p == 0 else lf.at[0, 0:NX])
+
+    update(3)
+    pl.semaphore_wait(barrier, (NY - 1) + (NZ - 1) + (NX - 1) + 1)
+    y_start(3, (1, 4))
     load_panel.wait()
+    send_panel(1)
+    update(2)
+    y_start(2, (1, 4))
+    y_start(3, (0, 3))
+    update(1)
+    y_start(1, (1, 4))
     at = pl.multiple_of(x * SUB, SUB)
     tiles = [lf[m, col, :, pl.ds(at, SUB)].astype(F32) for m in (0, 1)]
     turned = [pltpu.roll(tile, slab, 1) for tile in tiles]
@@ -149,97 +237,7 @@
     block = jnp.concatenate([jnp.where(even, tiles[0], turned[0]), jnp.where(even, turned[1], tiles[1])], axis=0)
     inverse = unit_inverse(block)
     dall[col] = inverse[:slab] + inverse[slab:]
-
-    for k in range(CHUNKS):
-        loads_b[k].wait()
-        bt[:, chunk * k : chunk * (k + 1)] = b_v[chunk * k : chunk * (k + 1), :].T
-
-    load(2).start()
-
-    pl.semaphore_wait(barrier, (NY - 1) + (NZ - 1) + (NX - 1) + 1)
-
-    def part(p, c):
-        return dall.at[c] if p == 0 else lf.at[(1, 0, 2)[p - 1], c]
-
-    def along_x(p, d):
-        return remote(part(p, col), part(p, col), px_s.at[p], px_r.at[p, d - 1], row, x_peer(d))
-
-    def across(p, d):
-        shard = part(p, lax.rem(x + NX - d, NX) * 2 + core)
-        return remote(shard, shard, pc_s.at[p], pc_r.at[p], row, other)
-
-    def send_panel(p):
-        for d in (2, 1, 3):
-            along_x(p, d).start()
-        across(p, 0).start()
-
     send_panel(0)
-    send_panel(1)
-
-    place[...] = jnp.zeros_like(place)
-    load_rhs.wait()
-    place[pl.ds(pl.multiple_of(z * (PIECE // NZ), 8), PIECE // NZ), :] = rhs_v[...]
-
-    def y_group(target):
-        return pl.multiple_of(target // NZ * group, group)
-
-    right_rows, left_rows = y_group(right), y_group(left)
-    far_rows = pl.multiple_of(lax.rem(y + 2, NY) * group, group)
-    own_rows = pl.multiple_of(y * group, group)
-
-    def y_copy(n, slot):
-        start = ((right_rows, 1), (far_rows, 0), (right_rows, 0), (left_rows, 0), (far_rows, 1), (left_rows, 1))[slot]
-        src = ut.at[n, pl.ds(start[0] + start[1] * half, half), :]
-        target = right if slot < 3 else left
-        return remote(src, yrecv.at[n, Y_SLOT[slot]], y_s, y_r.at[n, Y_SEM[slot]], target, col)
-
-    def y_start(n, slots):
-        for slot in slots:
-            y_copy(n, slot).start()
-
-    def update(n):
-        load(n).wait()
-        if n >= 2:
-            load(n - 2).start()
-        ut[n] = mm(bt[...], a_v[n])
-
-        @pl.when(n == y)
-        def _():
-            ut[n] = ut[n] - place[...].T
-
-    def relay(n):
-        all_here(y_r.at[n, 0], yrecv.at[n, 0])
-        ut[n, pl.ds(right_rows, half), :] += yrecv[n, 0]
-        y_copy(n, 2).start()
-        all_here(y_r.at[n, 1], yrecv.at[n, 1])
-        ut[n, pl.ds(left_rows + half, half), :] += yrecv[n, 1]
-        y_copy(n, 5).start()
-
-    def z_copy(n, d):
-        return remote(w.at[n, z_rows(0, d), :], zrecv.at[n, d - 1], z_s, z_r.at[n], z_peer(d), col)
-
-    def y_sum(n):
-        all_here(y_r.at[n, 2], yrecv.at[n, 2:6])
-        w[n, :half, :] = ut[n, pl.ds(own_rows, half), :] + (yrecv[n, 3] + yrecv[n, 4])
-        w[n, half:, :] = ut[n, pl.ds(own_rows + half, half), :] + (yrecv[n, 2] + yrecv[n, 5])
-        for d in Z_ORDER:
-            z_copy(n, d).start()
-
-    def forward(p):
-        for d in range(1, NX):
-            along_x(p, d).wait_recv()
-            across(p, d).start()
-
-    def arrived(p):
-        all_here(pc_r.at[p], dall.at[0:NX] if p == 0 else lf.at[0, 0:NX])
-
-    update(3)
-    y_start(3, (1, 4))
-    update(2)
-    y_start(2, (1, 4))
-    y_start(3, (0, 3))
-    update(1)
-    y_start(1, (1, 4))
     relay(3)
     y_start(2, (0, 3))
     update(0)
@@ -249,10 +247,10 @@
     send_panel(2)
     relay(1)
     y_start(0, (0, 3))
-    forward(0)
     forward(1)
     y_sum(3)
     relay(0)
+    forward(0)
     send_panel(3)
     y_sum(2)
     y_sum(1)

time: 41.4 us -> 40.9 us (0.988)
  Pallas kernels: 40.3 us -> 39.7 us
    pallas_call x1, Pallas kernels: 40.3 us -> 39.7 us  [shards(): pl.pallas_call(kernel, out_shape=jax.ShapeDtypeStruct((window, width), F3...]
where the time goes in v6:
time: 40.9 us; the launch traced here: 40.7 us
  Pallas kernels  39.7 us (97%)
  local copies, waits for them, and re-layouts  0.97 us (2%)
    pallas_call x1, Pallas kernels, shards(): pl.pallas_call(kernel, out_shape=jax.ShapeDtypeStruct((window, width), F3...  39.7 us
    unnamed x1, local copies, waits for them, and re-layouts  0.97 us

profile of v6, /device:TPU:8, one launch (start us, length us, event | category | flops | bytes accessed | tf_op | source)
XLA Modules:
  0.0 40.7 jit_solution(15199655057584794657)
XLA Ops:
  0.0 39.7 %shard_map.46 = f32[1024,256]{1,0:T(8,128)S(1)} custom-call(bf16[4096,1024]{1,0:T(8,128)(2,1)} %a_hbm.1, bf16[4096,256]{1,0:T(8,128)(2,1)} %b_hbm.1, f32[32,256]{1,0:T(8,128)} %rhs_hbm.1, bf16[3,64,512]{2,1,0:T(8,128)(2,1)} %panel_hbm.1), custom_call_target="tpu_custom_call" | custom-call | tf_op jit(solution)/shard_map/pallas_call | solution.py:420
  39.7 1.0 %copy.6 = f32[1024,256]{1,0:T(8,128)} copy(f32[1024,256]{1,0:T(8,128)S(1)} %shard_map.46) | data formatting | bytes 2097152

commit v7 on v6

--- a/solution.py
+++ b/solution.py
@@ -254,6 +254,7 @@
     send_panel(3)
     y_sum(2)
     y_sum(1)
+    forward(2)
 
     def whole_inverse(m):
         lane = lax.broadcasted_iota(jnp.int32, (slab, SUB), 1)
@@ -356,7 +357,6 @@
     arrived(1)
     whole_inverse(1)
     y_sum(0)
-    forward(2)
     second = solve(1, reduced(1))
     publish(1, second)
     forward(3)

time: 40.9 us -> 42.1 us (1.029)
  Pallas kernels: 39.7 us -> 41 us
    pallas_call x1, Pallas kernels: 39.7 us -> 41 us  [shards(): pl.pallas_call(kernel, out_shape=jax.ShapeDtypeStruct((window, width), F3...]
where the time goes in v7:
time: 42.1 us; the launch traced here: 42 us
  Pallas kernels  41 us (97%)
  local copies, waits for them, and re-layouts  0.97 us (2%)
    pallas_call x1, Pallas kernels, shards(): pl.pallas_call(kernel, out_shape=jax.ShapeDtypeStruct((window, width), F3...  41 us
    unnamed x1, local copies, waits for them, and re-layouts  0.97 us

profile of v7, /device:TPU:8, one launch (start us, length us, event | category | flops | bytes accessed | tf_op | source)
XLA Modules:
  0.0 42.0 jit_solution(2134010507648458347)
XLA Ops:
  0.0 41.0 %shard_map.46 = f32[1024,256]{1,0:T(8,128)S(1)} custom-call(bf16[4096,1024]{1,0:T(8,128)(2,1)} %a_hbm.1, bf16[4096,256]{1,0:T(8,128)(2,1)} %b_hbm.1, f32[32,256]{1,0:T(8,128)} %rhs_hbm.1, bf16[3,64,512]{2,1,0:T(8,128)(2,1)} %panel_hbm.1), custom_call_target="tpu_custom_call" | custom-call | tf_op jit(solution)/shard_map/pallas_call | solution.py:420
  41.0 1.0 %copy.6 = f32[1024,256]{1,0:T(8,128)} copy(f32[1024,256]{1,0:T(8,128)S(1)} %shard_map.46) | data formatting | bytes 2097152

commit v8 on v6

--- a/solution.py
+++ b/solution.py
@@ -244,9 +244,9 @@
     y_start(0, (1, 4))
     relay(2)
     y_start(1, (0, 3))
-    send_panel(2)
     relay(1)
     y_start(0, (0, 3))
+    send_panel(2)
     forward(1)
     y_sum(3)
     relay(0)

time: 40.9 us -> 40.9 us (level)
  no operation moved by 1% of the time
where the time goes in v8:
time: 40.9 us; the launch traced here: 40.8 us
  Pallas kernels  39.8 us (97%)
  local copies, waits for them, and re-layouts  0.97 us (2%)
    pallas_call x1, Pallas kernels, shards(): pl.pallas_call(kernel, out_shape=jax.ShapeDtypeStruct((window, width), F3...  39.8 us
    unnamed x1, local copies, waits for them, and re-layouts  0.97 us

profile of v8, /device:TPU:8, one launch (start us, length us, event | category | flops | bytes accessed | tf_op | source)
XLA Modules:
  0.0 40.8 jit_solution(8446086061146896345)
XLA Ops:
  0.0 39.8 %shard_map.46 = f32[1024,256]{1,0:T(8,128)S(1)} custom-call(bf16[4096,1024]{1,0:T(8,128)(2,1)} %a_hbm.1, bf16[4096,256]{1,0:T(8,128)(2,1)} %b_hbm.1, f32[32,256]{1,0:T(8,128)} %rhs_hbm.1, bf16[3,64,512]{2,1,0:T(8,128)(2,1)} %panel_hbm.1), custom_call_target="tpu_custom_call" | custom-call | tf_op jit(solution)/shard_map/pallas_call | solution.py:420
  39.8 1.0 %copy.6 = f32[1024,256]{1,0:T(8,128)} copy(f32[1024,256]{1,0:T(8,128)S(1)} %shard_map.46) | data formatting | bytes 2097152
